TPU v7x, 128 devices: a whole 4x4x4 slice. The times are simulated.
128 devices in a mesh: space: 16 (over z, x_lo, core), samp: 8 (over y, x_hi).
Axes of the slice: x: 4 (x_hi: 2, x_lo: 2; x = x_hi * 2 + x_lo), y: 4, z: 4, core: 2. Of those that a mesh axis runs over, the one named last changes fastest.
Arguments:
- basis_u: bfloat16 [128, 32, 8, 128], P('samp', 'space'), may hold values from -0.75 to 0.75
- basis_v: bfloat16 [128, 65536], P('space', 'samp'), may hold values from -0.75 to 0.75
- core_s: float32 [128, 128], replicated, may hold values from -4 to 4
- face_class: int32 [6, 32, 8, 128], P(None, 'space'), may hold values from 0 to 3
- sample_class: int32 [65536], P('samp'), may hold values from 0 to 3
Outputs:
- k_new: float32 [128, 32, 8, 128], P('samp', 'space')
- l_new: float32 [128, 65536], P('space', 'samp')
All inputs are finite; a program needn't handle non-finite values.
Results may differ from a plain program's by a relative error of at most 0.0046.
Values may be sent and summed in bfloat16 or wider, within the bound.
No kernel may reach another device: no remote copies, remote signals or barrier semaphores. Data moves between devices by JAX's collectives and lax.ppermute only.
A program may use at most 64 MiB of HBM per device.

v0:
```python
import jax
import jax.numpy as jnp
from jax import lax
from jax.sharding import PartitionSpec as P

step_size = 0.1


def padded(cells, sides, width):
    for axis, dim in sides:
        count = lax.axis_size(axis)
        ends = count - 1
        head = lax.slice_in_dim(cells, 0, width, axis=dim)
        tail = lax.slice_in_dim(cells, cells.shape[dim] - width, cells.shape[dim], axis=dim)
        cells = jnp.concatenate(
            [
                lax.ppermute(tail, axis, [(i, (i + 1) % count) for i in range(ends)]),
                cells,
                lax.ppermute(head, axis, [((i + 1) % count, i) for i in range(ends)]),
            ],
            axis=dim,
        )
    return cells


def with_core(factor, core_b):
    rank_size = core_b.shape[0]
    flat_rows = factor.reshape(rank_size, -1)
    product = lax.dot_general(
        core_b, flat_rows, (((0,), (0,)), ((), ())), preferred_element_type=jnp.float32
    ).astype(jnp.bfloat16)
    return product.reshape(factor.shape)


def diffuse(padded_k, face_class):
    weight = 0.25 * jnp.exp2(face_class.astype(jnp.float32))[:, None]
    padded_grid = jnp.pad(padded_k.astype(jnp.float32), ((0, 0), (0, 0), (1, 1), (1, 1)))
    centre = padded_grid[:, 1:-1, 1:-1, 1:-1]
    beside_all = (
        padded_grid[:, :-2, 1:-1, 1:-1],
        padded_grid[:, 2:, 1:-1, 1:-1],
        padded_grid[:, 1:-1, :-2, 1:-1],
        padded_grid[:, 1:-1, 2:, 1:-1],
        padded_grid[:, 1:-1, 1:-1, :-2],
        padded_grid[:, 1:-1, 1:-1, 2:],
    )
    summed = jnp.zeros_like(centre)
    for side_index in range(6):
        summed = summed + weight[side_index] * (beside_all[side_index] - centre)
    return summed


def per_device(basis_u, basis_v, core_s, face_class, sample_class):
    n_space = lax.axis_size("space")
    n_samp = lax.axis_size("samp")
    narrow, depth_x, rows_y, cols_z = basis_u.shape
    rank_size = core_s.shape[0]
    core_b = core_s.astype(jnp.bfloat16)
    full_u = lax.all_gather(basis_u, "samp", axis=0, tiled=True)
    k_old = with_core(full_u, core_b)
    padded_k = padded(k_old, (("space", 1),), 1)
    laplace = diffuse(padded_k, face_class)
    cells_total = depth_x * rows_y * cols_z * n_space
    samp_rows = basis_v.shape[1]
    samples_total = samp_rows * n_samp
    lane_width = rank_size // n_space
    full_v = lax.all_gather(basis_v, "space", axis=0, tiled=True)
    k_flat = k_old.reshape(rank_size, -1)
    u_rows = full_u.reshape(rank_size, -1)
    lap_b = laplace.reshape(rank_size, -1).astype(jnp.bfloat16)
    moment_part = lax.dot_general(
        u_rows, lap_b, (((1,), (1,)), ((), ())), preferred_element_type=jnp.float32
    )
    moment = lax.psum(moment_part, "space")
    growth = 0.5 + 0.5 * sample_class.astype(jnp.float32)
    block_rows = min(256, samp_rows)
    block_count = samp_rows // block_rows
    cell_weight = rank_size / cells_total

    def tile_terms(offset):
        v_block = lax.dynamic_slice_in_dim(full_v, offset, block_rows, 1)
        g_block = lax.dynamic_slice_in_dim(growth, offset, block_rows, 0)
        sample_field = lax.dot_general(
            k_flat, v_block, (((0,), (0,)), ((), ())), preferred_element_type=jnp.float32
        )
        reaction = (
            g_block[None, :] * sample_field - sample_field * sample_field * sample_field
        ).astype(jnp.bfloat16)
        onto_v = lax.dot_general(
            v_block, reaction, (((1,), (1,)), ((), ())), preferred_element_type=jnp.float32
        )
        onto_u = lax.dot_general(
            u_rows, reaction, (((1,), (0,)), ((), ())), preferred_element_type=jnp.float32
        )
        return (onto_v, onto_u * cell_weight)

    start_acc = jnp.zeros((rank_size, k_flat.shape[1]), jnp.float32)

    def turn_after(turn_index, state_pair):
        accumulated, l_terms = state_pair
        offset = turn_index * block_rows
        onto_v, l_term = tile_terms(offset)
        l_terms = lax.dynamic_update_slice_in_dim(l_terms, l_term, offset, 1)
        return (accumulated + onto_v, l_terms)

    start_terms = jnp.zeros((rank_size, samp_rows), jnp.float32)
    accumulated, l_terms = lax.fori_loop(0, block_count, turn_after, (start_acc, start_terms))
    l_proj = lax.psum_scatter(l_terms, "space", scatter_dimension=0, tiled=True)
    samp_offset = lax.axis_index("samp") * narrow
    k_term = accumulated.reshape(rank_size, depth_x, rows_y, cols_z)
    k_summed = lax.psum(k_term, "samp")
    k_proj = lax.dynamic_slice_in_dim(k_summed, samp_offset, narrow, 0)
    k_proj = k_proj * (rank_size / samples_total)
    k_mine = lax.dynamic_slice_in_dim(k_old, samp_offset, narrow, 0).astype(jnp.float32)
    lap_mine = lax.dynamic_slice_in_dim(laplace, samp_offset, narrow, 0)
    k_new = k_mine + step_size * (lap_mine + k_proj)
    lane_offset = lax.axis_index("space") * lane_width
    core_rows = lax.dynamic_slice_in_dim(core_b, lane_offset, lane_width, 0)
    l_old = jnp.dot(core_rows, full_v, preferred_element_type=jnp.float32)
    moment_rows = lax.dynamic_slice_in_dim(moment, lane_offset, lane_width, 0) * cell_weight
    side_term = jnp.dot(moment_rows, full_v.astype(jnp.float32), precision=lax.Precision.HIGHEST)
    l_new = l_old + step_size * (side_term + l_proj)
    return (k_new, l_new)


def solution(mesh):
    placed = (
        P("samp", "space", None, None),
        P("space", "samp"),
        P(),
        P(None, "space", None, None),
        P("samp"),
    )
    return jax.shard_map(
        per_device,
        mesh=mesh,
        in_specs=placed,
        out_specs=(P("samp", "space", None, None), P("space", "samp")),
        check_vma=False,
    )
```

profile of v0, /device:TPU:0, one launch (start us, length us, event | category | flops | bytes accessed | tf_op | source)
XLA Modules:
  0.0 497.0 jit_solution(16505963637963926047)
XLA Ops:
  8.8 37.5 %all_gather.6 = bf16[128,2,8,128]{3,2,1,0:T(8,128)(2,1)S(1)} all-gather(bf16[16,2,8,128]{3,2,1,0:T(8,128)(2,1)} %param.7), channel_id=1, replica_groups=mesh['space'=16,'samp'=8] {'samp'}, dimensions={0}, use_global_device_ids=true | all-gather | bytes 589824 | tf_op jit(solution)/shard_map/all_gather | solution.py:59
  49.4 1.3 collective-permute-start.1
  50.6 3.8 collective-permute-start
  55.2 2.4 broadcast_in_dim.11.clone
  57.6 155.9 %while.16 = (s32[]{:T(128)}, f32[128,2048]{1,0:T(8,128)S(1)}, f32[128,8192]{1,0:T(8,128)}, bf16[128,8192]{1,0:T(8,128)(2,1)}, f32[8192]{0:T(1024)}, /*index=5*/b...) while((s32[]{:T(128)}, f32[128,2048]{1,0:T(8,128)S(1)}, ...), condition=%wide.region_1.2_spmd.clone, body=%wide.region_0.1_spmd.clone.sunk | while | flops 405831680 | bytes 7081149 | solution.py:107
  58.4 1.6 fusion.58
  59.9 1.3 convolution_add_fusion.3
  63.2 1.6 fusion.58
  68.1 1.6 fusion.58
  69.7 1.3 convolution_add_fusion.3
  73.0 1.6 fusion.58
  74.6 1.3 convolution_add_fusion.3
  77.9 1.6 fusion.58
  79.5 1.3 convolution_add_fusion.3
  82.8 1.6 fusion.58
  84.4 1.3 convolution_add_fusion.3
  87.6 1.6 fusion.58
  89.2 1.3 convolution_add_fusion.3
  92.5 1.6 fusion.58
  94.1 1.3 convolution_add_fusion.3
  97.4 1.6 fusion.58
  99.0 1.3 convolution_add_fusion.3
  102.3 1.6 fusion.58
  103.9 1.3 convolution_add_fusion.3
  107.1 1.6 fusion.58
  112.0 1.6 fusion.58
  113.6 1.3 convolution_add_fusion.3
  116.8 1.6 fusion.58
  118.4 1.3 convolution_add_fusion.3
  121.7 1.6 fusion.58
  123.3 1.3 convolution_add_fusion.3
  126.6 1.6 fusion.58
  128.2 1.3 convolution_add_fusion.3
  131.4 1.6 fusion.58
  136.3 1.6 fusion.58
  137.9 1.3 convolution_add_fusion.3
  141.2 1.6 fusion.58
  142.8 1.3 convolution_add_fusion.3
  146.0 1.6 fusion.58
  150.9 1.6 fusion.58
  152.5 1.3 convolution_add_fusion.3
  155.8 1.6 fusion.58
  157.4 1.3 convolution_add_fusion.3
  160.6 1.6 fusion.58
  162.2 1.3 convolution_add_fusion.3
  165.5 1.6 fusion.58
  170.4 1.6 fusion.58
  172.0 1.3 convolution_add_fusion.3
  175.2 1.6 fusion.58
  180.1 1.6 fusion.58
  185.0 1.6 fusion.58
  186.6 1.3 convolution_add_fusion.3
  189.8 1.6 fusion.58
  194.7 1.6 fusion.58
  199.6 1.6 fusion.58
  204.5 1.6 fusion.58
  209.3 1.6 fusion.58
  210.9 1.3 convolution_add_fusion.3
  216.0 1.9 fusion.34
  221.6 86.1 %all-reduce.4.cloned.1.call-done = f32[128,2,8,128]{3,2,1,0:T(8,128)} async-done(((f32[128,2,8,128]{3,2,1,0:T(8,128)}), f32[128,2,8,128]{3,2,1,0:T(8,128)}) %all-reduce.4.cloned.1.call-update) | async-done | bytes 1048592 | tf_op jit(solution)/shard_map/psum | solution.py:111
  307.6 1.6 multiply_add_fusion
  309.3 106.7 %all-reduce.6.cloned.1.call-done = f32[128,128]{0,1:T(8,128)} async-done(((f32[128,128]{0,1:T(8,128)}), f32[128,128]{0,1:T(8,128)}) %all-reduce.6.cloned.1.call-update) | async-done | bytes 65552 | tf_op jit(solution)/shard_map/psum | solution.py:74
  416.0 71.8 %reduce-scatter.2.cloned.1.call-done = f32[8,8192]{1,0:T(8,128)} async-done(((f32[128,8192]{1,0:T(8,128)}), f32[8,8192]{1,0:T(8,128)}) %reduce-scatter.2.cloned.1.call-update) | async-done | bytes 262160 | tf_op jit(solution)/shard_map/reduce_scatter | solution.py:108
  487.7 2.7 fusion.8
  (175 shorter events, 88.8 us)
Async XLA Ops:
  7.2 48.0 %all-gather.2.cloned.1.call-start = ((), (), s32[]{:S(2)}) async-start(), calls=%async_computation.1 | async-start | bytes 2228224 | tf_op jit(solution)/shard_map/all_gather | solution.py:67
  7.9 299.7 %all-reduce.4.cloned.1.call-start = ((), (), s32[]{:S(2)}) async-start(), calls=%async_computation.2 | async-start | bytes 2097152 | tf_op jit(solution)/shard_map/psum | solution.py:111
  8.8 38.6 %copy-start.3 = (bf16[128,128]{1,0:T(8,128)(2,1)}, bf16[128,128]{1,0:T(8,128)(2,1)S(1)}, u32[]{:S(2)}) copy-start(bf16[128,128]{1,0:T(8,128)(2,1)S(1)} %convert_element_type.32) | copy-start | bytes 98308
  46.2 8.3 %copy-start.1 = (bf16[128,2,8,128]{3,2,1,0:T(8,128)(2,1)}, bf16[128,2,8,128]{3,2,1,0:T(8,128)(2,1)S(1)}, u32[]{:S(2)}) copy-start(bf16[128,2,8,128]{3,2,1,0:T(8,128)(2,1)S(1)} %all_gather.6) | copy-start | bytes 1572868
  46.2 8.3 %copy-start.5 = (s32[8192]{0:T(1024)S(1)}, s32[8192]{0:T(1024)}, u32[]{:S(2)}) copy-start(s32[8192]{0:T(1024)} %param.11) | copy-start | bytes 98308
  49.4 165.4 %collective-permute-start.1 = (bf16[128,1,8,128]{3,2,1,0:T(8,128)(2,1)}, bf16[128,1,8,128]{3,2,1,0:T(8,128)(2,1)S(1)}, u32[]{:S(2)}, u32[]{:S(2)}) collective-permute-start(bf16[128,1,8,128]{3,2,1,0:T(8,128)(2,1)} %get-tuple-element.170), channel_id=1, source_target_pairs={{8,0},{16,8},{24,16},{32,24},{40,32},{48,40},{56,48},{64,56},{72,6... | collective-permute-start | bytes 786440 | tf_op jit(solution)/shard_map/ppermute | solution.py:19
  50.6 164.1 %collective-permute-start = (bf16[128,1,8,128]{3,2,1,0:T(8,128)(2,1)}, bf16[128,1,8,128]{3,2,1,0:T(8,128)(2,1)}, u32[]{:S(2)}, u32[]{:S(2)}) collective-permute-start(bf16[128,1,8,128]{3,2,1,0:T(8,128)(2,1)} %get-tuple-element.169), channel_id=1, source_target_pairs={{0,8},{8,16},{16,24},{24,32},{32,40},{40,48},{48,56},{56,64},{64,7... | collective-permute-start | bytes 786440 | tf_op jit(solution)/shard_map/ppermute | solution.py:17
  213.5 1.3 copy-start.4
  214.7 201.3 %all-reduce.6.cloned.1.call-start = ((), (), s32[]{:S(2)}) async-start(), calls=%async_computation.3 | async-start | bytes 131072 | tf_op jit(solution)/shard_map/psum | solution.py:74
  216.0 1.9 copy-start.2
  218.9 268.8 %reduce-scatter.2.cloned.1.call-start = ((), (), s32[]{:S(2)}) async-start(), calls=%async_computation.4 | async-start | bytes 4456448 | tf_op jit(solution)/shard_map/reduce_scatter | solution.py:108
  218.9 1.6 copy-start
Sparse Core Ops, SparseCore 0:
  9.7 37.1 all-gather.1
  214.8 92.7 all-reduce.3
  310.7 105.2 all-reduce.5
  418.2 69.4 reduce-scatter.1
where the time goes:
time: 501 us; the launch traced here: 497 us
  waiting for transfers between devices  266 us (53%)
  matrix products  111 us (22%)
  local copies, waits for them, and re-layouts  56 us (11%)
  blocking collectives  37.5 us (7%)
  between operations  13.9 us (3%)
  other arithmetic  6.25 us (1%)
  starting transfers between devices  5.2 us (1%)
    psum x1, waiting for transfers between devices, per_device(): moment = lax.psum(moment_part, 'space')  107 us
    psum x1, waiting for transfers between devices, per_device(): k_summed = lax.psum(k_term, 'samp')  86.1 us
    reduce_scatter x1, waiting for transfers between devices, per_device(): l_proj = lax.psum_scatter(l_terms, 'space', scatter_dimension=0, tiled=True)  71.8 us
    dot_general x32, matrix products, tile_terms(): lax.dot_general(k_flat, v_block, (((0,), (0,)), ((), ())), preferred_elem...  50.6 us
    dot_general x32, matrix products, tile_terms(): lax.dot_general(v_block, reaction, (((1,), (1,)), ((), ())), preferred_el...  40.9 us
    all_gather x1, blocking collectives, per_device(): full_u = lax.all_gather(basis_u, 'samp', axis=0, tiled=True)  37.5 us
    dynamic_update_slice x64, local copies, waits for them, and re-layouts, turn_after(): l_terms = lax.dynamic_update_slice_in_dim(l_terms, l_term, offset, 1)  24.9 us
    dynamic_slice x32, local copies, waits for them, and re-layouts, tile_terms(): g_block = lax.dynamic_slice_in_dim(growth, offset, block_rows, 0)  24.3 us
  transfers between devices with their start and end apart: 6, of which 3 were waited for; matrix products, arithmetic and copies ran while one was open for 34% of the time, Pallas kernels for 0%

commit v1 on v0

--- a/solution.py
+++ b/solution.py
@@ -108,7 +108,7 @@
     l_proj = lax.psum_scatter(l_terms, "space", scatter_dimension=0, tiled=True)
     samp_offset = lax.axis_index("samp") * narrow
     k_term = accumulated.reshape(rank_size, depth_x, rows_y, cols_z)
-    k_summed = lax.psum(k_term, "samp")
+    k_summed = jnp.sum(lax.all_gather(k_term, "samp"), axis=0)
     k_proj = lax.dynamic_slice_in_dim(k_summed, samp_offset, narrow, 0)
     k_proj = k_proj * (rank_size / samples_total)
     k_mine = lax.dynamic_slice_in_dim(k_old, samp_offset, narrow, 0).astype(jnp.float32)

time: 501 us -> 389 us (0.78)
  waiting for transfers between devices: 266 us -> 185 us
  local copies, waits for them, and re-layouts: 56 us -> 33.1 us
  matrix products: 111 us -> 102 us
    psum x1, waiting for transfers between devices: 107 us -> 0.01 us  [per_device(): moment = lax.psum(moment_part, 'space')]
    all_gather x0 -> x1, waiting for transfers between devices: none -> 105 us  [per_device(): k_summed = jnp.sum(lax.all_gather(k_term, 'samp'), axis=0)]
    psum x1 -> x0, waiting for transfers between devices: 86.1 us -> none  [per_device(): k_summed = lax.psum(k_term, 'samp')]
    dynamic_slice x32, local copies, waits for them, and re-layouts: 24.3 us -> 2.49 us  [tile_terms(): g_block = lax.dynamic_slice_in_dim(growth, offset, block_rows, 0)]
    dot_general x32, matrix products: 50.6 us -> 42.8 us  [tile_terms(): lax.dot_general(k_flat, v_block, (((0,), (0,)), ((), ())), preferred_elem...]
  transfers between devices with their start and end apart: 6 -> 6, of which waited for: 3 -> 3; matrix products, arithmetic and copies ran while one was open for 34% -> 36% of each run, Pallas kernels for 0% -> 0%
where the time goes in v1:
time: 389 us; the launch traced here: 385 us
  waiting for transfers between devices  185 us (48%)
  matrix products  102 us (26%)
  blocking collectives  37.5 us (10%)
  local copies, waits for them, and re-layouts  33.1 us (9%)
  between operations  13.9 us (4%)
  other arithmetic  9.56 us (2%)
    all_gather x1, waiting for transfers between devices, per_device(): k_summed = jnp.sum(lax.all_gather(k_term, 'samp'), axis=0)  105 us
    reduce_scatter x1, waiting for transfers between devices, per_device(): l_proj = lax.psum_scatter(l_terms, 'space', scatter_dimension=0, tiled=True)  75.4 us
    dot_general x32, matrix products, tile_terms(): lax.dot_general(k_flat, v_block, (((0,), (0,)), ((), ())), preferred_elem...  42.8 us
    dot_general x32, matrix products, tile_terms(): lax.dot_general(v_block, reaction, (((1,), (1,)), ((), ())), preferred_el...  40.7 us
    all_gather x1, blocking collectives, per_device(): full_u = lax.all_gather(basis_u, 'samp', axis=0, tiled=True)  37.5 us
    dynamic_update_slice x64, local copies, waits for them, and re-layouts, turn_after(): l_terms = lax.dynamic_update_slice_in_dim(l_terms, l_term, offset, 1)  25.1 us
    dot_general x32, matrix products, tile_terms(): lax.dot_general(u_rows, reaction, (((1,), (0,)), ((), ())), preferred_ele...  13.9 us
  transfers between devices with their start and end apart: 6, of which 3 were waited for; matrix products, arithmetic and copies ran while one was open for 36% of the time, Pallas kernels for 0%

profile of v1, /device:TPU:0, one launch (start us, length us, event | category | flops | bytes accessed | tf_op | source)
XLA Modules:
  0.0 385.4 jit_solution(14308192738715752003)
XLA Ops:
  8.8 37.5 %all_gather.9 = bf16[128,2,8,128]{3,2,1,0:T(8,128)(2,1)S(1)} all-gather(bf16[16,2,8,128]{3,2,1,0:T(8,128)(2,1)} %param.7), channel_id=1, replica_groups=mesh['space'=16,'samp'=8] {'samp'}, dimensions={0}, use_global_device_ids=true | all-gather | bytes 589824 | tf_op jit(solution)/shard_map/all_gather | solution.py:59
  47.6 1.3 collective-permute-start
  48.9 1.3 collective-permute-start.1
  50.4 4.0 %collective-permute-done.1 = bf16[128,1,8,128]{3,2,1,0:T(8,128)(2,1)} collective-permute-done((bf16[128,1,8,128]{3,2,1,0:T(8,128)(2,1)}, bf16[128,1,8,128]{3,2,1,0:T(8,128)(2,1)}, u32[]{:S(2)}, u32[]{:S(2)}) %collective-permute-start.1) | collective-permute-done | bytes 262176 | tf_op jit(solution)/shard_map/ppermute | solution.py:19
  55.7 1.8 fusion.34
  58.6 2.4 broadcast_in_dim.11.clone
  61.0 126.7 %while.16 = (s32[]{:T(128)}, f32[128,2048]{1,0:T(8,128)S(1)}, f32[128,8192]{1,0:T(8,128)}, bf16[128,8192]{1,0:T(8,128)(2,1)}, f32[8192]{0:T(1024)S(1)}, /*index=...) while((s32[]{:T(128)}, f32[128,2048]{1,0:T(8,128)S(1)}, ...), condition=%wide.region_1.2_spmd.clone, body=%wide.region_0.1_spmd.clone.sunk | while | flops 405831680 | bytes 7081141 | solution.py:107
  61.1 1.3 fusion.58
  63.6 1.3 convolution_add_fusion.3
  65.0 1.3 fusion.58
  69.0 1.3 fusion.58
  72.9 1.3 fusion.58
  75.5 1.3 convolution_add_fusion.3
  76.9 1.3 fusion.58
  79.5 1.3 convolution_add_fusion.3
  80.9 1.3 fusion.58
  83.4 1.3 convolution_add_fusion.3
  84.8 1.3 fusion.58
  87.4 1.3 convolution_add_fusion.3
  88.8 1.3 fusion.58
  91.4 1.3 convolution_add_fusion.3
  92.8 1.3 fusion.58
  95.3 1.3 convolution_add_fusion.3
  96.7 1.3 fusion.58
  99.3 1.3 convolution_add_fusion.3
  100.7 1.3 fusion.58
  103.3 1.3 convolution_add_fusion.3
  104.7 1.3 fusion.58
  108.6 1.3 fusion.58
  111.2 1.3 convolution_add_fusion.3
  112.6 1.3 fusion.58
  116.6 1.3 fusion.58
  120.5 1.3 fusion.58
  123.1 1.3 convolution_add_fusion.3
  124.5 1.3 fusion.58
  127.0 1.3 convolution_add_fusion.3
  128.4 1.3 fusion.58
  131.0 1.3 convolution_add_fusion.3
  132.4 1.3 fusion.58
  136.3 1.3 fusion.58
  140.3 1.3 fusion.58
  144.2 1.3 fusion.58
  146.8 1.3 convolution_add_fusion.3
  148.2 1.3 fusion.58
  150.7 1.3 convolution_add_fusion.3
  152.1 1.3 fusion.58
  156.1 1.3 fusion.58
  158.7 1.3 convolution_add_fusion.3
  160.0 1.3 fusion.58
  164.0 1.3 fusion.58
  167.9 1.3 fusion.58
  170.5 1.3 convolution_add_fusion.3
  171.9 1.3 fusion.58
  174.5 1.3 convolution_add_fusion.3
  175.8 1.3 fusion.58
  179.8 1.3 fusion.58
  182.4 1.3 convolution_add_fusion.3
  183.8 1.3 fusion.58
  186.4 1.3 convolution_add_fusion.3
  190.0 75.4 %reduce-scatter.2.cloned.1.call-done = f32[8,8192]{1,0:T(8,128)} async-done(((f32[128,8192]{1,0:T(8,128)}), f32[8,8192]{1,0:T(8,128)}) %reduce-scatter.2.cloned.1.call-update) | async-done | bytes 262160 | tf_op jit(solution)/shard_map/reduce_scatter | solution.py:108
  265.4 2.7 fusion.8
  268.1 105.0 %all-gather.5.cloned.1.call-done = f32[8,128,2,8,128]{4,3,2,1,0:T(8,128)} async-done(((f32[1,128,2,8,128]{4,3,2,1,0:T(8,128)}), f32[8,128,2,8,128]{4,3,2,1,0:T(8,128)}) %all-gather.5.cloned.1.call-update) | async-done | bytes 8388624 | tf_op jit(solution)/shard_map/all_gather | solution.py:111
  373.2 4.1 %reduce_sum.9 = f32[128,2,8,128]{3,2,1,0:T(8,128)S(1)} reduce(f32[8,128,2,8,128]{4,3,2,1,0:T(8,128)} %all-gather.5.cloned.1.call-done, f32[]{:T(128)} %constant.61.clone.1), dimensions={0}, to_apply=%region_2.3 | reduce | flops 1835008 | bytes 9437188 | tf_op jit(solution)/shard_map/reduce_sum | solution.py:111
  377.2 1.6 multiply_add_fusion
  (172 shorter events, 64.4 us)
Async XLA Ops:
  7.2 43.0 %copy-start.2 = (s32[6,2,8,128]{3,2,1,0:T(8,128)S(1)}, s32[6,2,8,128]{3,2,1,0:T(8,128)}, u32[]{:S(2)}) copy-start(s32[6,2,8,128]{3,2,1,0:T(8,128)} %param.10) | copy-start | bytes 147460
  7.2 51.4 %all-gather.3.cloned.1.call-start = ((), (), s32[]{:S(2)}) async-start(), calls=%async_computation.1 | async-start | bytes 2228224 | tf_op jit(solution)/shard_map/all_gather | solution.py:67
  7.9 182.1 %all-reduce.3.cloned.1.call-start = ((), (), s32[]{:S(2)}) async-start(), calls=%async_computation.3 | async-start | bytes 131072 | tf_op jit(solution)/shard_map/psum | solution.py:74
  46.3 4.1 %copy-start.3 = (s32[8192]{0:T(1024)S(1)}, s32[8192]{0:T(1024)}, u32[]{:S(2)}) copy-start(s32[8192]{0:T(1024)} %param.11) | copy-start | bytes 98308
  46.7 9.0 %copy-start.1 = (bf16[16,8,16,128]{3,2,1,0:T(8,128)(2,1)}, bf16[16,8,16,128]{3,2,1,0:T(8,128)(2,1)S(1)}, u32[]{:S(2)}) copy-start(bf16[16,8,16,128]{3,2,1,0:T(8,128)(2,1)S(1)} %copy.17) | copy-start | bytes 1572868
  47.6 2.8 collective-permute-start
  48.9 5.6 %collective-permute-start.1 = (bf16[128,1,8,128]{3,2,1,0:T(8,128)(2,1)}, bf16[128,1,8,128]{3,2,1,0:T(8,128)(2,1)}, u32[]{:S(2)}, u32[]{:S(2)}) collective-permute-start(bf16[128,1,8,128]{3,2,1,0:T(8,128)(2,1)} %get-tuple-element.170), channel_id=1, source_target_pairs={{8,0},{16,8},{24,16},{32,24},{40,32},{48,40},{56,48},{64,56},{72,6... | collective-permute-start | bytes 786440 | tf_op jit(solution)/shard_map/ppermute | solution.py:19
  58.5 206.9 %reduce-scatter.2.cloned.1.call-start = ((), (), s32[]{:S(2)}) async-start(), calls=%async_computation.4 | async-start | bytes 4456448 | tf_op jit(solution)/shard_map/reduce_scatter | solution.py:108
  187.7 2.0 copy-start
  187.7 185.5 %all-gather.5.cloned.1.call-start = ((), (), s32[]{:S(2)}) async-start(), calls=%async_computation.2 | async-start | bytes 9437184 | tf_op jit(solution)/shard_map/all_gather | solution.py:111
Sparse Core Ops, SparseCore 0:
  9.7 37.1 all-gather.2
  58.6 114.0 all-reduce.2
  187.8 77.5 reduce-scatter.1
  267.6 105.5 all-gather.4
